TPU v7x, 128 devices: a whole 4x4x4 slice. The times are simulated.
128 devices in a mesh: section: 8 (over x, core), mat: 16 (over y, z).
Axes of the slice: x: 4, y: 4, z: 4, core: 2. Of those that a mesh axis runs over, the one named last changes fastest.
Arguments:
- eigvec: bfloat16 [8, 3072, 3072], P('section')
- eig_level: float32 [8, 3072], P('section'), may hold values from 0.5 to 5
- energies: float32 [2], replicated, may hold values from -0.3 to 0.45
- order: int32 [2], replicated, may hold values from 0 to 1, each once
- init_r: bfloat16 [2, 3072, 3072], P(None, 'mat')
Outputs:
- boundary_r: bfloat16 [8, 2, 3072, 3072], P('section', None, 'mat')
Inputs may be any that keep to these rules, and one draw needn't show every extreme that they name: order holds each of 0 to 1 once.
All inputs are finite; a program needn't handle non-finite values.
Results may differ from a plain program's by a relative error of at most 0.0064.
Values may be sent and summed in bfloat16 or wider, within the bound.
A program may use at most 128 MiB of HBM per device.

v0:
```python
import jax
import jax.numpy as jnp
from jax import lax
from jax.sharding import PartitionSpec as P

MB = 1
MICROS = 2


sector_width = 1.0


def from_behind(value, axis, steps):
    count = lax.axis_size(axis)
    first, last = (max(0, -steps), min(count, count - steps))
    return lax.ppermute(value, axis, [(source, source + steps) for source in range(first, last)])


def greens(levels, energy):
    wave_number = jnp.sqrt(levels - energy)
    phase_arg = wave_number * sector_width
    sinh_value = jnp.sinh(phase_arg)
    g_one = jnp.cosh(phase_arg) / (wave_number * sinh_value)
    g_two = 1.0 / (wave_number * sinh_value)
    return (g_one, g_two)


def on_device(eigvec, eig_level, energies, order, init_r):
    sector_vecs = eigvec[0]
    levels = eig_level[0]
    row_count = init_r.shape[1]
    chan_count = init_r.shape[2]
    slot_total = energies.shape[0]
    section_id = lax.axis_index("section")
    mat_id = lax.axis_index("mat")
    tick_count = lax.axis_size("section") + MICROS - 1
    row_start = mat_id * row_count
    square_eye = jnp.eye(row_count, dtype=jnp.float32)
    block_shape = (MB, row_count, chan_count)

    def tick(tick_index, state_pair):
        outgoing, results = state_pair
        received = from_behind(outgoing, "section", 1)
        micro_index = tick_index - section_id
        active = (micro_index >= 0) & (micro_index < MICROS)
        micro_slot = jnp.clip(micro_index, 0, MICROS - 1)
        picked = lax.dynamic_slice_in_dim(order, micro_slot * MB, MB)
        initial = jnp.take(init_r, picked, axis=0)
        r_now = jnp.where(section_id == 0, initial, received)
        g_one, g_two = greens(levels[None, :], jnp.take(energies, picked)[:, None])
        half_left = lax.cond(
            active,
            lambda matrix: jnp.einsum(
                "eck,ka->eca", matrix, sector_vecs, preferred_element_type=jnp.float32
            ).astype(jnp.bfloat16),
            lambda matrix: jnp.zeros(block_shape, jnp.bfloat16),
            r_now,
        )
        left_cols = lax.all_to_all(half_left, "mat", split_axis=2, concat_axis=1, tiled=True)
        r_inner = lax.cond(
            active,
            lambda matrix: jnp.einsum(
                "eca,cb->eab", matrix, sector_vecs, preferred_element_type=jnp.float32
            ),
            lambda matrix: jnp.zeros(block_shape, jnp.float32),
            left_cols,
        )
        local_square = lax.dynamic_slice_in_dim(r_inner, row_start, row_count, 2)
        local_diag = jnp.diagonal(local_square, axis1=1, axis2=2)
        full_diag = lax.all_gather(local_diag, "mat", axis=1, tiled=True)
        precond = 1.0 / (g_one + jnp.abs(full_diag))
        side = g_two * precond
        diag_term = g_one - 2.0 * g_two * g_two * precond + g_one * side * side
        side_rows = lax.dynamic_slice_in_dim(side, row_start, row_count, 1)
        term_rows = lax.dynamic_slice_in_dim(diag_term, row_start, row_count, 1)
        scaled = side_rows[:, :, None] * r_inner * side[:, None, :]
        square_part = lax.dynamic_slice_in_dim(scaled, row_start, row_count, 2)
        square_part = square_part + term_rows[:, :, None] * square_eye[None]
        r_outer = lax.dynamic_update_slice_in_dim(scaled, square_part, row_start, 2).astype(
            jnp.bfloat16
        )
        half_right = lax.cond(
            active,
            lambda matrix: jnp.einsum(
                "eab,kb->eak", matrix, sector_vecs, preferred_element_type=jnp.float32
            ).astype(jnp.bfloat16),
            lambda matrix: jnp.zeros(block_shape, jnp.bfloat16),
            r_outer,
        )
        right_cols = lax.all_to_all(half_right, "mat", split_axis=2, concat_axis=1, tiled=True)
        r_next = lax.cond(
            active,
            lambda matrix: jnp.einsum(
                "eak,ja->ekj", matrix, sector_vecs, preferred_element_type=jnp.float32
            ).astype(jnp.bfloat16),
            lambda matrix: jnp.zeros(block_shape, jnp.bfloat16),
            right_cols,
        )
        current = lax.dynamic_slice_in_dim(results, micro_slot * MB, MB, 0)
        chosen = jnp.where(active, r_next, current)
        results = lax.dynamic_update_slice_in_dim(results, chosen, micro_slot * MB, 0)
        return (r_next, results)

    start_pair = (
        jnp.zeros(block_shape, jnp.bfloat16),
        jnp.zeros((slot_total, row_count, chan_count), jnp.bfloat16),
    )
    final_pair = lax.fori_loop(0, tick_count, tick, start_pair)
    return final_pair[1][None]


def solution(mesh):
    in_specs = (P("section", None, None), P("section", None), P(), P(), P(None, "mat", None))
    out_specs = P("section", None, "mat", None)
    return jax.shard_map(
        on_device, mesh=mesh, in_specs=in_specs, out_specs=out_specs, check_vma=False
    )
```

profile of v0, /device:TPU:7, one launch (start us, length us, event | category | flops | bytes accessed | tf_op | source)
XLA Modules:
  0.0 2405.8 jit_solution(8141285315022421023)
XLA Ops:
  2.9 2402.9 %while.20 = (s32[]{:T(128)}, bf16[1,192,3072]{2,1,0:T(8,128)(2,1)}, bf16[2,192,3072]{2,1,0:T(8,128)(2,1)}, s32[]{:T(128)}, s32[2]{0:T(128)S(1)}, /*index=5*/f32[...) while((s32[]{:T(128)}, bf16[1,192,3072]{2,1,0:T(8,128)(2,1)}, ...), condition=%wide.region_9.10_spmd.clone, body=%wide.region_0.9_spmd.clone.sunk | while | flops 14501033984 | bytes 163839632 | solution.py:108
  17.3 18.3 reduce.4
  81.8 56.7 %all-reduce.3 = f32[3072]{0:T(1024)S(1)} all-reduce(f32[3072]{0:T(1024)S(1)} %dynamic-update-slice.5), channel_id=2, replica_groups=mesh['section'=8,'mat'=16] {'mat'}, use_global_device_ids=true, to_apply=%add | all-reduce | flops 3072 | bytes 24576 | tf_op jit(solution)/shard_map/while
  151.9 18.3 reduce.5
  216.7 30.6 %collective-permute-done = bf16[1,192,3072]{2,1,0:T(8,128)(2,1)S(1)} collective-permute-done((bf16[1,192,3072]{2,1,0:T(8,128)(2,1)}, bf16[1,192,3072]{2,1,0:T(8,128)(2,1)S(1)}, u32[]{:S(2)}, u32[]{:S(2)}) %collective-permute-start) | collective-permute-done | bytes 1179680 | tf_op jit(solution)/shard_map/while/body/eval_jaxpr/ppermute | solution.py:16
  256.7 18.3 reduce.4
  317.6 56.4 %all-reduce.3 = f32[3072]{0:T(1024)S(1)} all-reduce(f32[3072]{0:T(1024)S(1)} %dynamic-update-slice.5), channel_id=2, replica_groups=mesh['section'=8,'mat'=16] {'mat'}, use_global_device_ids=true, to_apply=%add | all-reduce | flops 3072 | bytes 24576 | tf_op jit(solution)/shard_map/while
  387.5 18.3 reduce.5
  452.3 30.6 %collective-permute-done = bf16[1,192,3072]{2,1,0:T(8,128)(2,1)S(1)} collective-permute-done((bf16[1,192,3072]{2,1,0:T(8,128)(2,1)}, bf16[1,192,3072]{2,1,0:T(8,128)(2,1)S(1)}, u32[]{:S(2)}, u32[]{:S(2)}) %collective-permute-start) | collective-permute-done | bytes 1179680 | tf_op jit(solution)/shard_map/while/body/eval_jaxpr/ppermute | solution.py:16
  492.2 18.3 reduce.4
  553.2 56.4 %all-reduce.3 = f32[3072]{0:T(1024)S(1)} all-reduce(f32[3072]{0:T(1024)S(1)} %dynamic-update-slice.5), channel_id=2, replica_groups=mesh['section'=8,'mat'=16] {'mat'}, use_global_device_ids=true, to_apply=%add | all-reduce | flops 3072 | bytes 24576 | tf_op jit(solution)/shard_map/while
  623.0 18.3 reduce.5
  687.8 30.6 %collective-permute-done = bf16[1,192,3072]{2,1,0:T(8,128)(2,1)S(1)} collective-permute-done((bf16[1,192,3072]{2,1,0:T(8,128)(2,1)}, bf16[1,192,3072]{2,1,0:T(8,128)(2,1)S(1)}, u32[]{:S(2)}, u32[]{:S(2)}) %collective-permute-start) | collective-permute-done | bytes 1179680 | tf_op jit(solution)/shard_map/while/body/eval_jaxpr/ppermute | solution.py:16
  727.8 18.3 reduce.4
  788.7 56.4 %all-reduce.3 = f32[3072]{0:T(1024)S(1)} all-reduce(f32[3072]{0:T(1024)S(1)} %dynamic-update-slice.5), channel_id=2, replica_groups=mesh['section'=8,'mat'=16] {'mat'}, use_global_device_ids=true, to_apply=%add | all-reduce | flops 3072 | bytes 24576 | tf_op jit(solution)/shard_map/while
  858.6 18.3 reduce.5
  923.4 30.6 %collective-permute-done = bf16[1,192,3072]{2,1,0:T(8,128)(2,1)S(1)} collective-permute-done((bf16[1,192,3072]{2,1,0:T(8,128)(2,1)}, bf16[1,192,3072]{2,1,0:T(8,128)(2,1)S(1)}, u32[]{:S(2)}, u32[]{:S(2)}) %collective-permute-start) | collective-permute-done | bytes 1179680 | tf_op jit(solution)/shard_map/while/body/eval_jaxpr/ppermute | solution.py:16
  963.3 18.3 reduce.4
  1024.3 56.4 %all-reduce.3 = f32[3072]{0:T(1024)S(1)} all-reduce(f32[3072]{0:T(1024)S(1)} %dynamic-update-slice.5), channel_id=2, replica_groups=mesh['section'=8,'mat'=16] {'mat'}, use_global_device_ids=true, to_apply=%add | all-reduce | flops 3072 | bytes 24576 | tf_op jit(solution)/shard_map/while
  1094.1 18.3 reduce.5
  1158.9 30.6 %collective-permute-done = bf16[1,192,3072]{2,1,0:T(8,128)(2,1)S(1)} collective-permute-done((bf16[1,192,3072]{2,1,0:T(8,128)(2,1)}, bf16[1,192,3072]{2,1,0:T(8,128)(2,1)S(1)}, u32[]{:S(2)}, u32[]{:S(2)}) %collective-permute-start) | collective-permute-done | bytes 1179680 | tf_op jit(solution)/shard_map/while/body/eval_jaxpr/ppermute | solution.py:16
  1198.8 18.3 reduce.4
  1259.8 56.4 %all-reduce.3 = f32[3072]{0:T(1024)S(1)} all-reduce(f32[3072]{0:T(1024)S(1)} %dynamic-update-slice.5), channel_id=2, replica_groups=mesh['section'=8,'mat'=16] {'mat'}, use_global_device_ids=true, to_apply=%add | all-reduce | flops 3072 | bytes 24576 | tf_op jit(solution)/shard_map/while
  1394.5 30.6 %collective-permute-done = bf16[1,192,3072]{2,1,0:T(8,128)(2,1)S(1)} collective-permute-done((bf16[1,192,3072]{2,1,0:T(8,128)(2,1)}, bf16[1,192,3072]{2,1,0:T(8,128)(2,1)S(1)}, u32[]{:S(2)}, u32[]{:S(2)}) %collective-permute-start) | collective-permute-done | bytes 1179680 | tf_op jit(solution)/shard_map/while/body/eval_jaxpr/ppermute | solution.py:16
  1434.4 18.3 reduce.4
  1495.4 56.3 %all-reduce.3 = f32[3072]{0:T(1024)S(1)} all-reduce(f32[3072]{0:T(1024)S(1)} %dynamic-update-slice.5), channel_id=2, replica_groups=mesh['section'=8,'mat'=16] {'mat'}, use_global_device_ids=true, to_apply=%add | all-reduce | flops 3072 | bytes 24576 | tf_op jit(solution)/shard_map/while
  1629.9 229.7 %collective-permute-done = bf16[1,192,3072]{2,1,0:T(8,128)(2,1)S(1)} collective-permute-done((bf16[1,192,3072]{2,1,0:T(8,128)(2,1)}, bf16[1,192,3072]{2,1,0:T(8,128)(2,1)S(1)}, u32[]{:S(2)}, u32[]{:S(2)}) %collective-permute-start) | collective-permute-done | bytes 1179680 | tf_op jit(solution)/shard_map/while/body/eval_jaxpr/ppermute | solution.py:16
  1879.4 18.3 reduce.4
  1950.4 56.4 %all-reduce.3 = f32[3072]{0:T(1024)S(1)} all-reduce(f32[3072]{0:T(1024)S(1)} %dynamic-update-slice.5), channel_id=2, replica_groups=mesh['section'=8,'mat'=16] {'mat'}, use_global_device_ids=true, to_apply=%add | all-reduce | flops 3072 | bytes 24576 | tf_op jit(solution)/shard_map/while
  2106.4 47.7 %collective-permute-done = bf16[1,192,3072]{2,1,0:T(8,128)(2,1)S(1)} collective-permute-done((bf16[1,192,3072]{2,1,0:T(8,128)(2,1)}, bf16[1,192,3072]{2,1,0:T(8,128)(2,1)S(1)}, u32[]{:S(2)}, u32[]{:S(2)}) %collective-permute-start) | collective-permute-done | bytes 1179680 | tf_op jit(solution)/shard_map/while/body/eval_jaxpr/ppermute | solution.py:16
  2173.8 18.3 reduce.4
  2248.2 59.2 %all-reduce.3 = f32[3072]{0:T(1024)S(1)} all-reduce(f32[3072]{0:T(1024)S(1)} %dynamic-update-slice.5), channel_id=2, replica_groups=mesh['section'=8,'mat'=16] {'mat'}, use_global_device_ids=true, to_apply=%add | all-reduce | flops 3072 | bytes 24576 | tf_op jit(solution)/shard_map/while
  (478 shorter events, 1246.7 us)
Async XLA Ops:
  2.9 5.1 collective-permute-start
  40.3 20.4 all-to-all-start
  79.4 59.3 %copy-start = (f32[1,192,3072]{2,1,0:T(8,128)}, f32[1,192,3072]{2,1,0:T(8,128)S(1)}, u32[]{:S(2)}) copy-start(f32[1,192,3072]{2,1,0:T(8,128)S(1)} %get-tuple-element.599) | copy-start | bytes 7077892 | tf_op jit(solution)/shard_map/while
  174.9 16.9 all-to-all-start.1
  213.2 34.1 %collective-permute-start = (bf16[1,192,3072]{2,1,0:T(8,128)(2,1)}, bf16[1,192,3072]{2,1,0:T(8,128)(2,1)S(1)}, u32[]{:S(2)}, u32[]{:S(2)}) collective-permute-start(bf16[1,192,3072]{2,1,0:T(8,128)(2,1)} %get-tuple-element.549), channel_id=1, source_target_pairs={{0,16},{16,32},{32,48},{48,64},{64,80},{80,96},{96,112},{1,17},{17... | collective-permute-start | bytes 3538952 | tf_op jit(solution)/shard_map/while/body/eval_jaxpr/ppermute | solution.py:16
  279.7 16.9 all-to-all-start
  315.3 59.0 %copy-start = (f32[1,192,3072]{2,1,0:T(8,128)}, f32[1,192,3072]{2,1,0:T(8,128)S(1)}, u32[]{:S(2)}) copy-start(f32[1,192,3072]{2,1,0:T(8,128)S(1)} %get-tuple-element.599) | copy-start | bytes 7077892 | tf_op jit(solution)/shard_map/while
  410.5 16.9 all-to-all-start.1
  448.8 34.1 %collective-permute-start = (bf16[1,192,3072]{2,1,0:T(8,128)(2,1)}, bf16[1,192,3072]{2,1,0:T(8,128)(2,1)S(1)}, u32[]{:S(2)}, u32[]{:S(2)}) collective-permute-start(bf16[1,192,3072]{2,1,0:T(8,128)(2,1)} %get-tuple-element.549), channel_id=1, source_target_pairs={{0,16},{16,32},{32,48},{48,64},{64,80},{80,96},{96,112},{1,17},{17... | collective-permute-start | bytes 3538952 | tf_op jit(solution)/shard_map/while/body/eval_jaxpr/ppermute | solution.py:16
  515.2 16.9 all-to-all-start
  550.8 59.0 %copy-start = (f32[1,192,3072]{2,1,0:T(8,128)}, f32[1,192,3072]{2,1,0:T(8,128)S(1)}, u32[]{:S(2)}) copy-start(f32[1,192,3072]{2,1,0:T(8,128)S(1)} %get-tuple-element.599) | copy-start | bytes 7077892 | tf_op jit(solution)/shard_map/while
  646.0 16.9 all-to-all-start.1
  684.3 34.1 %collective-permute-start = (bf16[1,192,3072]{2,1,0:T(8,128)(2,1)}, bf16[1,192,3072]{2,1,0:T(8,128)(2,1)S(1)}, u32[]{:S(2)}, u32[]{:S(2)}) collective-permute-start(bf16[1,192,3072]{2,1,0:T(8,128)(2,1)} %get-tuple-element.549), channel_id=1, source_target_pairs={{0,16},{16,32},{32,48},{48,64},{64,80},{80,96},{96,112},{1,17},{17... | collective-permute-start | bytes 3538952 | tf_op jit(solution)/shard_map/while/body/eval_jaxpr/ppermute | solution.py:16
  750.8 16.9 all-to-all-start
  786.4 59.0 %copy-start = (f32[1,192,3072]{2,1,0:T(8,128)}, f32[1,192,3072]{2,1,0:T(8,128)S(1)}, u32[]{:S(2)}) copy-start(f32[1,192,3072]{2,1,0:T(8,128)S(1)} %get-tuple-element.599) | copy-start | bytes 7077892 | tf_op jit(solution)/shard_map/while
  881.5 16.9 all-to-all-start.1
  919.9 34.1 %collective-permute-start = (bf16[1,192,3072]{2,1,0:T(8,128)(2,1)}, bf16[1,192,3072]{2,1,0:T(8,128)(2,1)S(1)}, u32[]{:S(2)}, u32[]{:S(2)}) collective-permute-start(bf16[1,192,3072]{2,1,0:T(8,128)(2,1)} %get-tuple-element.549), channel_id=1, source_target_pairs={{0,16},{16,32},{32,48},{48,64},{64,80},{80,96},{96,112},{1,17},{17... | collective-permute-start | bytes 3538952 | tf_op jit(solution)/shard_map/while/body/eval_jaxpr/ppermute | solution.py:16
  986.3 16.9 all-to-all-start
  1117.1 16.9 all-to-all-start.1
  1155.4 34.1 %collective-permute-start = (bf16[1,192,3072]{2,1,0:T(8,128)(2,1)}, bf16[1,192,3072]{2,1,0:T(8,128)(2,1)S(1)}, u32[]{:S(2)}, u32[]{:S(2)}) collective-permute-start(bf16[1,192,3072]{2,1,0:T(8,128)(2,1)} %get-tuple-element.549), channel_id=1, source_target_pairs={{0,16},{16,32},{32,48},{48,64},{64,80},{80,96},{96,112},{1,17},{17... | collective-permute-start | bytes 3538952 | tf_op jit(solution)/shard_map/while/body/eval_jaxpr/ppermute | solution.py:16
  1221.8 16.9 all-to-all-start
  1352.6 16.9 all-to-all-start.1
  1391.0 34.1 %collective-permute-start = (bf16[1,192,3072]{2,1,0:T(8,128)(2,1)}, bf16[1,192,3072]{2,1,0:T(8,128)(2,1)S(1)}, u32[]{:S(2)}, u32[]{:S(2)}) collective-permute-start(bf16[1,192,3072]{2,1,0:T(8,128)(2,1)} %get-tuple-element.549), channel_id=1, source_target_pairs={{0,16},{16,32},{32,48},{48,64},{64,80},{80,96},{96,112},{1,17},{17... | collective-permute-start | bytes 3538952 | tf_op jit(solution)/shard_map/while/body/eval_jaxpr/ppermute | solution.py:16
  1457.4 16.9 all-to-all-start
  1588.1 16.9 all-to-all-start.1
  1626.4 233.2 %collective-permute-start = (bf16[1,192,3072]{2,1,0:T(8,128)(2,1)}, bf16[1,192,3072]{2,1,0:T(8,128)(2,1)S(1)}, u32[]{:S(2)}, u32[]{:S(2)}) collective-permute-start(bf16[1,192,3072]{2,1,0:T(8,128)(2,1)} %get-tuple-element.549), channel_id=1, source_target_pairs={{0,16},{16,32},{32,48},{48,64},{64,80},{80,96},{96,112},{1,17},{17... | collective-permute-start | bytes 3538952 | tf_op jit(solution)/shard_map/while/body/eval_jaxpr/ppermute | solution.py:16
  1902.4 16.9 all-to-all-start
  2053.4 16.9 all-to-all-start.1
  2102.9 51.2 %collective-permute-start = (bf16[1,192,3072]{2,1,0:T(8,128)(2,1)}, bf16[1,192,3072]{2,1,0:T(8,128)(2,1)S(1)}, u32[]{:S(2)}, u32[]{:S(2)}) collective-permute-start(bf16[1,192,3072]{2,1,0:T(8,128)(2,1)} %get-tuple-element.549), channel_id=1, source_target_pairs={{0,16},{16,32},{32,48},{48,64},{64,80},{80,96},{96,112},{1,17},{17... | collective-permute-start | bytes 3538952 | tf_op jit(solution)/shard_map/while/body/eval_jaxpr/ppermute | solution.py:16
  2196.8 20.3 all-to-all-start
  2245.9 61.8 %copy-start = (f32[1,192,3072]{2,1,0:T(8,128)}, f32[1,192,3072]{2,1,0:T(8,128)S(1)}, u32[]{:S(2)}) copy-start(f32[1,192,3072]{2,1,0:T(8,128)S(1)} %get-tuple-element.599) | copy-start | bytes 7077892 | tf_op jit(solution)/shard_map/while
  2354.0 19.2 all-to-all-start.1
  (44 other events, 316.5 us)
where the time goes:
time: 2420 us; the launch traced here: 2410 us
  waiting for transfers between devices  670 us (28%)
  local copies, waits for them, and re-layouts  643 us (27%)
  blocking collectives  511 us (21%)
  other arithmetic  378 us (16%)
  starting transfers between devices  94.1 us (4%)
  matrix products  81.4 us (3%)
  loops' own time  29.1 us (1%)
    while x9, blocking collectives  511 us
    ppermute x9, waiting for transfers between devices, from_behind(): lax.ppermute(value, axis, [(source, source + steps) for source in range(f...  463 us
    while x18, other arithmetic  330 us
    while x171, local copies, waits for them, and re-layouts  271 us
    all_to_all x9, waiting for transfers between devices, tick(): lax.all_to_all(half_right, 'mat', split_axis=2, concat_axis=1, tiled=True)  115 us
    all_to_all x9, waiting for transfers between devices, tick(): lax.all_to_all(half_left, 'mat', split_axis=2, concat_axis=1, tiled=True)  92.3 us
    all_to_all x18, local copies, waits for them, and re-layouts, tick(): lax.all_to_all(half_left, 'mat', split_axis=2, concat_axis=1, tiled=True)  91.1 us
    all_to_all x18, local copies, waits for them, and re-layouts, tick(): lax.all_to_all(half_right, 'mat', split_axis=2, concat_axis=1, tiled=True)  82.2 us
  transfers between devices with their start and end apart: 27, of which 27 were waited for; matrix products, arithmetic and copies ran while one was open for 1% of the time, Pallas kernels for 0%

commit v1 on v0

v1 whole, which is shorter than its diff:
```python
import functools

import jax
import jax.numpy as jnp
from jax import lax
from jax.experimental import pallas as pl
from jax.experimental.pallas import tpu as pltpu
from jax.sharding import PartitionSpec as P

MESH = pl.DeviceIdType.MESH
SIDE = 4
MATS = SIDE * SIDE
MAIN = 128
sector_width = 1.0


def greens(levels, energy):
    wave_number = jnp.sqrt(levels - energy)
    phase_arg = wave_number * sector_width
    sinh_value = jnp.sinh(phase_arg)
    g_one = jnp.cosh(phase_arg) / (wave_number * sinh_value)
    g_two = 1.0 / (wave_number * sinh_value)
    return (g_one, g_two)


def kernel(
    sections,
    eig_ref, g_one_ref, g_two_ref, init_ref, out_ref,
    vecs, vecs_t, rmat, inner, outer, half_lhs, send, recv, diag_send, diag_recv, side_ref,
    load_sem, init_sem, out_sem, send_sem, recv_sem, diag_send_sem, diag_recv_sem,
    pass_send_sem, pass_recv_sem,
):
    nch = vecs.shape[0]
    rows = rmat.shape[1]
    rest = rows - MAIN
    tall = rows // 2
    half = nch // 2
    tile = rows * SIDE
    win = 2 * rows
    f32, bf16 = jnp.float32, jnp.bfloat16

    section = lax.axis_index("section")
    me = lax.axis_index("mat")
    y, z = me // SIDE, me % SIDE
    odd = me % 2
    y_order = [(y + 2) % SIDE, SIDE - 1 - y, y + 1 - 2 * (y % 2), y]
    own_half = y // 2
    far_half = 1 - own_half

    def load(h):
        part = pl.ds(h * half, half)
        return pltpu.make_async_copy(eig_ref.at[0, part], vecs.at[part], load_sem.at[h])

    for h in range(2):
        load(h).start()

    def row_copies(slot):
        first = pl.multiple_of(odd * rest, rest)
        second = pl.multiple_of(MAIN * (1 - odd), rest)
        return ((pl.ds(first, MAIN), pl.ds(0, MAIN)), (pl.ds(second, rest), pl.ds(MAIN, rest)))

    def init_copies(slot):
        return [
            pltpu.make_async_copy(init_ref.at[slot, a], rmat.at[slot, b], init_sem.at[slot, n])
            for n, (a, b) in enumerate(row_copies(slot))
        ]

    def out_copies(slot):
        return [
            pltpu.make_async_copy(rmat.at[slot, b], out_ref.at[0, slot, a], out_sem.at[slot, n])
            for n, (a, b) in enumerate(row_copies(slot))
        ]

    @pl.when(section == 0)
    def _():
        for slot in range(2):
            for copy in init_copies(slot):
                copy.start()

    barrier = pltpu.get_barrier_semaphore()

    @pl.loop(0, MATS)
    def _(peer):
        @pl.when(peer != me)
        def _():
            pl.semaphore_signal(barrier, inc=1, device_id=(section, peer), device_id_type=MESH)

    @pl.when(section > 0)
    def _():
        pl.semaphore_signal(barrier, inc=1, device_id=(section - 1, me), device_id_type=MESH)

    @pl.when(section < sections - 1)
    def _():
        pl.semaphore_signal(barrier, inc=1, device_id=(section + 1, me), device_id_type=MESH)

    has_last = (section + sections - 1) // sections
    has_next = (2 * sections - 2 - section) // sections
    pl.semaphore_wait(barrier, MATS - 1 + has_last + has_next)

    lane = lax.broadcasted_iota(jnp.int32, (tall, MAIN), 1)
    low = lane < rest
    row_id = lax.broadcasted_iota(jnp.int32, (rows, win), 0)
    col_id = lax.broadcasted_iota(jnp.int32, (rows, win), 1)
    target = jnp.where(odd == 0, row_id, jnp.where(row_id < MAIN, row_id + win - MAIN, row_id + rest))
    on_diag = col_id == target
    win_cols = pl.ds(pl.multiple_of((me // 2) * win, MAIN), win)

    def transpose_vecs():
        @pl.loop(0, nch // MAIN)
        def _(r):
            part = pl.ds(pl.multiple_of(r * MAIN, MAIN), MAIN)
            vecs_t[:, part] = vecs[part, :].T

    def block_copy(trip, slot, place, dest):
        return pltpu.make_async_remote_copy(
            src_ref=send.at[slot, place],
            dst_ref=recv.at[trip, slot, me],
            send_sem=send_sem.at[slot, place],
            recv_sem=recv_sem.at[trip, slot, me],
            device_id=(section, dest),
            device_id_type=MESH,
        )

    def block_arrival(trip, slot, source):
        return pltpu.make_async_remote_copy(
            src_ref=send.at[slot, 0],
            dst_ref=recv.at[trip, slot, source],
            send_sem=send_sem.at[slot, 0],
            recv_sem=recv_sem.at[trip, slot, source],
            device_id=(section, source),
            device_id_type=MESH,
        )

    def ship(trip, slot, step, value):
        main_t = value[:MAIN].T
        rest_t = value[rest:].T
        for j in range(SIDE):
            base = rows * j
            if j % 2 == 0:
                main = main_t[base:base + rows]
                top = rest_t[base:base + tall]
                bottom = rest_t[base + tall:base + rows]
            else:
                main = jnp.concatenate([main_t[base + rest:base + rows], main_t[base:base + rest]], 0)
                top = rest_t[base + rest:base + rest + tall]
                bottom = jnp.concatenate([rest_t[base + rest + tall:base + rows], rest_t[base:base + rest]], 0)
            packed = jnp.where(low, pltpu.roll(top, rest, 1), bottom)
            place = SIDE * step + j
            send[slot, place, :rows] = main.astype(bf16)
            send[slot, place, rows:] = packed.astype(bf16)
        for j in range(SIDE):
            place = SIDE * step + j
            dest = y_order[step] * SIDE + j
            if step < SIDE - 1:
                block_copy(trip, slot, place, dest).start()
            else:
                @pl.when(j != z)
                def _():
                    block_copy(trip, slot, place, dest).start()
        if step == SIDE - 1:
            recv[trip, slot, me] = send[slot, SIDE * step + z]

    def wait_sent(trip, slot):
        for place in range(MATS):
            dest = y_order[place // SIDE] * SIDE + place % SIDE
            if place < MATS - SIDE:
                block_copy(trip, slot, place, dest).wait_send()
            else:
                @pl.when(place % SIDE != z)
                def _():
                    block_copy(trip, slot, place, dest).wait_send()

    def gather_half(trip, slot, which, own):
        for n in range(MATS // 2):
            source = which * (MATS // 2) + n
            if own:
                @pl.when(source != me)
                def _():
                    block_arrival(trip, slot, source).wait_recv()
            else:
                block_arrival(trip, slot, source).wait_recv()
        for q in range(MATS // 4):
            even = which * (MATS // 2) + 2 * q
            base = win * q
            half_lhs[:, base:base + MAIN] = recv[trip, slot, even, :rows]
            half_lhs[:, base + 2 * MAIN:base + 3 * MAIN] = recv[trip, slot, even + 1, :rows]
            left = recv[trip, slot, even, rows:].astype(f32)
            right = recv[trip, slot, even + 1, rows:].astype(f32)
            top = jnp.where(low, left, pltpu.roll(right, rest, 1))
            bottom = jnp.where(low, pltpu.roll(left, rest, 1), right)
            half_lhs[:tall, base + MAIN:base + 2 * MAIN] = top.astype(bf16)
            half_lhs[tall:, base + MAIN:base + 2 * MAIN] = bottom.astype(bf16)

    def dot(a, b):
        return jnp.dot(a, b, preferred_element_type=f32)

    def half_rows(which):
        return pl.ds(pl.multiple_of(which * half, MAIN), half)

    def pass_copy(slot, n):
        part = pl.ds(n * tile, tile)
        return pltpu.make_async_remote_copy(
            src_ref=rmat.at[slot, :, part],
            dst_ref=rmat.at[slot, :, part],
            send_sem=pass_send_sem.at[slot, n],
            recv_sem=pass_recv_sem.at[slot, n],
            device_id=(section + 1, me),
            device_id_type=MESH,
        )

    def pass_arrival(slot, n):
        part = pl.ds(n * tile, tile)
        return pltpu.make_async_remote_copy(
            src_ref=rmat.at[slot, :, part],
            dst_ref=rmat.at[slot, :, part],
            send_sem=pass_send_sem.at[slot, n],
            recv_sem=pass_recv_sem.at[slot, n],
            device_id=(section - 1, me),
            device_id_type=MESH,
        )

    def left_half(slot):
        @pl.when(section == 0)
        def _():
            for copy in init_copies(slot):
                copy.wait()

        for h in range(2):
            @pl.when(section > 0)
            def _():
                for n in range(2 * h, 2 * h + 2):
                    pass_arrival(slot, n).wait_recv()

            if h == 0:
                for n in range(2):
                    cols = slice(n * half, (n + 1) * half)
                    inner[slot, :, cols] = dot(rmat[slot, :, :half], vecs[:half, cols])
        for step in range(SIDE):
            cols = pl.ds(pl.multiple_of(y_order[step] * tile, MAIN), tile)
            value = inner[slot, :, cols] + dot(rmat[slot, :, half:], vecs[half:, cols])
            ship(0, slot, step, value)

    def diag_copy(slot, dest):
        return pltpu.make_async_remote_copy(
            src_ref=diag_send.at[slot],
            dst_ref=diag_recv.at[slot, me],
            send_sem=diag_send_sem.at[slot, dest],
            recv_sem=diag_recv_sem.at[slot, me],
            device_id=(section, dest),
            device_id_type=MESH,
        )

    def diag_arrival(slot, source):
        return pltpu.make_async_remote_copy(
            src_ref=diag_send.at[slot],
            dst_ref=diag_recv.at[slot, source],
            send_sem=diag_send_sem.at[slot, source],
            recv_sem=diag_recv_sem.at[slot, source],
            device_id=(section, source),
            device_id_type=MESH,
        )

    def inner_product(slot):
        gather_half(0, slot, far_half, False)
        for n in range(2):
            cols = slice(n * half, (n + 1) * half)
            inner[slot, :, cols] = dot(half_lhs[...], vecs[half_rows(far_half), cols])
        gather_half(0, slot, own_half, True)
        for n in range(2):
            cols = slice(n * half, (n + 1) * half)
            inner[slot, :, cols] += dot(half_lhs[...], vecs[half_rows(own_half), cols])
        mine = jnp.sum(jnp.where(on_diag, inner[slot, :, win_cols], 0.0), axis=0, keepdims=True)
        diag_send[slot] = jnp.zeros(diag_send.shape[1:], f32)
        for n in range(win // MAIN):
            diag_send[slot, n:n + 1, :] = mine[:, n * MAIN:(n + 1) * MAIN]
        diag_recv[slot, me] = diag_send[slot]

        @pl.loop(0, MATS)
        def _(dest):
            @pl.when(dest != me)
            def _():
                diag_copy(slot, dest).start()

    def right_half(slot):
        @pl.loop(0, MATS)
        def _(source):
            @pl.when(source != me)
            def _():
                diag_arrival(slot, source).wait_recv()

        pieces = []
        for p in range(MATS // 2):
            pair = diag_recv[slot, 2 * p] + diag_recv[slot, 2 * p + 1]
            pieces += [pair[n:n + 1, :] for n in range(win // MAIN)]
        full_diag = jnp.concatenate(pieces, axis=1)
        g_one = g_one_ref[slot:slot + 1, :]
        g_two = g_two_ref[slot:slot + 1, :]
        precond = 1.0 / (g_one + jnp.abs(full_diag))
        side = g_two * precond
        term = g_one - 2.0 * g_two * g_two * precond + g_one * side * side
        side_ref[0:1, :] = side
        side_ref[1:2, :] = term
        side_win = side_ref[0:1, win_cols]
        term_win = side_ref[1:2, win_cols]
        side_rows = jnp.sum(jnp.where(on_diag, side_win, 0.0), axis=1, keepdims=True)
        for q in range(nch // win):
            cols = slice(q * win, (q + 1) * win)
            outer[:, cols] = (side_rows * inner[slot, :, cols] * side[:, cols]).astype(bf16)
        scaled = side_rows * inner[slot, :, win_cols] * side_win
        outer[:, win_cols] = (scaled + jnp.where(on_diag, term_win, 0.0)).astype(bf16)
        wait_sent(0, slot)
        for step in range(SIDE):
            cols = pl.ds(pl.multiple_of(y_order[step] * tile, MAIN), tile)
            ship(1, slot, step, dot(outer[...], vecs_t[:, cols]))

    def next_rows(slot):
        gather_half(1, slot, far_half, False)
        for n in range(2):
            cols = slice(n * half, (n + 1) * half)
            inner[slot, :, cols] = dot(half_lhs[...], vecs_t[half_rows(far_half), cols])
        gather_half(1, slot, own_half, True)
        for n in range(SIDE):
            cols = slice(n * tile, (n + 1) * tile)
            value = inner[slot, :, cols] + dot(half_lhs[...], vecs_t[half_rows(own_half), cols])
            rmat[slot, :, cols] = value.astype(bf16)

            @pl.when(section < sections - 1)
            def _():
                pass_copy(slot, n).start()
        for copy in out_copies(slot):
            copy.start()

    for h in range(2):
        load(h).wait()

    @pl.when(section > 0)
    def _():
        transpose_vecs()

    left_half(0)

    @pl.when(section == 0)
    def _():
        transpose_vecs()

    inner_product(0)
    left_half(1)
    right_half(0)
    inner_product(1)
    next_rows(0)
    right_half(1)
    next_rows(1)

    for slot in range(2):
        wait_sent(1, slot)
        for copy in out_copies(slot):
            copy.wait()

        @pl.loop(0, MATS)
        def _(dest):
            @pl.when(dest != me)
            def _():
                diag_copy(slot, dest).wait_send()

        @pl.when(section < sections - 1)
        def _():
            for n in range(SIDE):
                pass_copy(slot, n).wait_send()


def on_device(sections, eigvec, eig_level, energies, order, init_r):
    nch = eigvec.shape[1]
    rows = init_r.shape[1]
    g_one, g_two = greens(eig_level[0][None, :], jnp.take(energies, order)[:, None])
    initial = jnp.take(init_r, order, axis=0)
    any_spec = pl.BlockSpec(memory_space=pl.ANY)
    vmem_spec = pl.BlockSpec(memory_space=pltpu.VMEM)
    dma = pltpu.SemaphoreType.DMA
    bf16, f32 = jnp.bfloat16, jnp.float32
    block = rows + rows // 2
    return pl.pallas_call(
        functools.partial(kernel, sections),
        out_shape=jax.ShapeDtypeStruct((1, 2, rows, nch), bf16),
        in_specs=[any_spec, vmem_spec, vmem_spec, any_spec],
        out_specs=any_spec,
        scratch_shapes=[
            pltpu.VMEM((nch, nch), bf16),
            pltpu.VMEM((nch, nch), bf16),
            pltpu.VMEM((2, rows, nch), bf16),
            pltpu.VMEM((2, rows, nch), f32),
            pltpu.VMEM((rows, nch), bf16),
            pltpu.VMEM((rows, nch // 2), bf16),
            pltpu.VMEM((2, MATS, block, MAIN), bf16),
            pltpu.VMEM((2, 2, MATS, block, MAIN), bf16),
            pltpu.VMEM((2, 8, MAIN), f32),
            pltpu.VMEM((2, MATS, 8, MAIN), f32),
            pltpu.VMEM((2, nch), f32),
            dma((2,)),
            dma((2, 2)),
            dma((2, 2)),
            dma((2, MATS)),
            dma((2, 2, MATS)),
            dma((2, MATS)),
            dma((2, MATS)),
            dma((2, SIDE)),
            dma((2, SIDE)),
        ],
        compiler_params=pltpu.CompilerParams(
            collective_id=0, has_side_effects=True, vmem_limit_bytes=67043328
        ),
        name="sectors",
    )(eigvec, g_one, g_two, initial)


def solution(mesh):
    in_specs = (P("section", None, None), P("section", None), P(), P(), P(None, "mat", None))
    out_specs = P("section", None, "mat", None)
    return jax.shard_map(
        functools.partial(on_device, mesh.shape["section"]),
        mesh=mesh, in_specs=in_specs, out_specs=out_specs, check_vma=False,
    )
```

time: 2420 us -> 457 us (0.19)
  waiting for transfers between devices: 670 us -> 0 us
  local copies, waits for them, and re-layouts: 643 us -> 6.88 us
  blocking collectives: 511 us -> 0 us
  Pallas kernels: 0 us -> 445 us
  other arithmetic: 378 us -> 4.54 us
  starting transfers between devices: 94.1 us -> 0 us
  matrix products: 81.4 us -> 0 us
  loops' own time: 29.1 us -> 0 us
    while x9 -> x0, blocking collectives: 511 us -> none
    ppermute x9 -> x0, waiting for transfers between devices: 463 us -> none  [from_behind(): lax.ppermute(value, axis, [(source, source + steps) for source in range(f...]
    pallas_call x0 -> x1, Pallas kernels: none -> 445 us  [on_device(): pl.pallas_call(functools.partial(kernel, sections), out_shape=jax.ShapeDt...]
    while x18 -> x0, other arithmetic: 330 us -> none
    while x171 -> x0, local copies, waits for them, and re-layouts: 271 us -> none
    all_to_all x18 -> x0, waiting for transfers between devices: 207 us -> none  [the longest x9 115 us: tick(): lax.all_to_all(half_right, 'mat', split_axis=2, concat_axis=1, tiled=True)]
    all_to_all x36 -> x0, local copies, waits for them, and re-layouts: 173 us -> none  [the longest x18 91.1 us: tick(): lax.all_to_all(half_left, 'mat', split_axis=2, concat_axis=1, tiled=True)]
    cond x18 -> x0, local copies, waits for them, and re-layouts: 136 us -> none  [the longest x9 67.9 us: tick(): lax.cond(active, lambda matrix: jnp.einsum('eck,ka->eca', matrix, sector_...]
  transfers between devices with their start and end apart: 27 -> 0, of which waited for: 27 -> 0; matrix products, arithmetic and copies ran while one was open for 1% -> 0% of each run, Pallas kernels for 0% -> 0%
where the time goes in v1:
time: 457 us
  Pallas kernels  445 us (97%)
  local copies, waits for them, and re-layouts  6.88 us (2%)
    pallas_call x1, Pallas kernels, on_device(): pl.pallas_call(functools.partial(kernel, sections), out_shape=jax.ShapeDt...  445 us

profile of v1, /device:TPU:7, one launch (start us, length us, event | category | flops | bytes accessed | tf_op | source)
XLA Modules:
  0.0 456.7 jit_solution(10993771389695927848)
XLA Ops:
  0.0 0.7 compare_select_fusion.1
  0.7 1.3 gather_fusion
  2.0 0.7 broadcast_select_fusion.1
  2.6 1.5 broadcast_divide_fusion
  4.1 2.4 gather_fusion.1
  6.5 1.7 broadcast_select_fusion.init_ref
  8.2 445.3 %sectors.1 = bf16[1,2,192,3072]{3,2,1,0:T(8,128)(2,1)} custom-call(bf16[1,3072,3072]{2,1,0:T(8,128)(2,1)} %eig_ref.1, f32[2,3072]{1,0:T(2,128)} %get-tuple-element.8.g_one_ref, f32[2,3072]{1,0:T(2,128)} %get-tuple-element.7.g_two_ref, bf16[2,192,3072]{2,1,0:T(8,128)(2,1)} %broadcast_select_fusion.init_ref), custom_call_target="tpu_custom_call" | custom-call | tf_op jit(solution)/shard_map/sectors/pallas_call | solution.py:381
  453.5 3.2 copy.7
  (1 shorter events, 0.0 us)

commit v2 on v1

--- a/solution.py
+++ b/solution.py
@@ -12,6 +12,35 @@
 MATS = SIDE * SIDE
 MAIN = 128
 sector_width = 1.0
+
+
+LEFT, INNER, PROPAGATE, RIGHT, NEXT, FLIP_OUT, FLIP_IN, TURN = range(8)
+FIRST = [
+    (LEFT, 0), (TURN, 0), (INNER, 0), (TURN, 1), (PROPAGATE, 0), (RIGHT, 0), (LEFT, 1),
+    (NEXT, 0), (INNER, 1), (PROPAGATE, 1), (RIGHT, 1), (NEXT, 1),
+]
+CHAIN = [
+    (LEFT, 0), (INNER, 0), (PROPAGATE, 0), (LEFT, 1), (INNER, 1), (PROPAGATE, 1),
+]
+PLAIN = CHAIN + [(RIGHT, 0), (RIGHT, 1), (NEXT, 0), (NEXT, 1)]
+FLIPPED = CHAIN + [
+    (FLIP_OUT, 0), (FLIP_OUT, 1), (FLIP_IN, 0), (RIGHT, 0), (FLIP_IN, 1), (RIGHT, 1),
+    (NEXT, 0), (NEXT, 1),
+]
+LAST = [
+    (LEFT, 0), (INNER, 0), (PROPAGATE, 0), (LEFT, 1), (RIGHT, 0), (INNER, 1), (NEXT, 0),
+    (PROPAGATE, 1), (RIGHT, 1), (NEXT, 1),
+]
+STEPS, BASE, DIGITS = 14, 17, 7
+
+
+def digits(order):
+    codes = [2 * stage + slot for stage, slot in order]
+    codes += [BASE - 1] * (STEPS - len(codes))
+    return [
+        sum(code * BASE ** n for n, code in enumerate(codes[part:part + DIGITS]))
+        for part in (0, DIGITS)
+    ]
 
 
 def greens(levels, energy):
@@ -28,7 +57,8 @@
     eig_ref, g_one_ref, g_two_ref, init_ref, out_ref,
     vecs, vecs_t, rmat, inner, outer, half_lhs, send, recv, diag_send, diag_recv, side_ref,
     load_sem, init_sem, out_sem, send_sem, recv_sem, diag_send_sem, diag_recv_sem,
-    pass_send_sem, pass_recv_sem,
+    pass_send_sem, pass_recv_sem, slice_send_sem, slice_recv_sem, stream_send_sem, stream_recv_sem,
+    ring_send_sem, ring_recv_sem, ready_sem, go_sem,
 ):
     nch = vecs.shape[0]
     rows = rmat.shape[1]
@@ -47,12 +77,33 @@
     own_half = y // 2
     far_half = 1 - own_half
 
-    def load(h):
+    even_section = section % 2 == 0
+    flipped = even_section & (section >= 2)
+    last = sections - 1
+    f_dot = functools.partial(jnp.dot, preferred_element_type=f32)
+
+    def load(h, space):
         part = pl.ds(h * half, half)
-        return pltpu.make_async_copy(eig_ref.at[0, part], vecs.at[part], load_sem.at[h])
-
-    for h in range(2):
-        load(h).start()
+        return pltpu.make_async_copy(eig_ref.at[0, part], space.at[part], load_sem.at[h])
+
+    def load_too(h):
+        part = pl.ds(h * half, half)
+        return pltpu.make_async_copy(eig_ref.at[0, part], vecs.at[part], load_sem.at[2 + h])
+
+    @pl.when(even_section)
+    def _():
+        for h in range(2):
+            load(h, vecs).start()
+
+    @pl.when(section % 2 == 1)
+    def _():
+        for h in range(2):
+            load(h, vecs_t).start()
+
+    @pl.when(section == 1)
+    def _():
+        for h in range(2):
+            load_too(h).start()
 
     def row_copies(slot):
         first = pl.multiple_of(odd * rest, rest)
@@ -105,11 +156,184 @@
     on_diag = col_id == target
     win_cols = pl.ds(pl.multiple_of((me // 2) * win, MAIN), win)
 
-    def transpose_vecs():
+    def transpose_chunk(q):
+        cols = pl.ds(pl.multiple_of(q * win, MAIN), win)
+
         @pl.loop(0, nch // MAIN)
         def _(r):
             part = pl.ds(pl.multiple_of(r * MAIN, MAIN), MAIN)
-            vecs_t[:, part] = vecs[part, :].T
+            vecs_t[cols, part] = vecs[part, cols].T
+
+    def transpose_in_place(block=256):
+        @pl.loop(0, nch // block)
+        def _(i):
+            @pl.loop(i, nch // block)
+            def _(j):
+                a = pl.ds(pl.multiple_of(i * block, block), block)
+                b = pl.ds(pl.multiple_of(j * block, block), block)
+                upper = vecs_t[a, b].T
+                lower = vecs_t[b, a].T
+                vecs_t[b, a] = upper
+                vecs_t[a, b] = lower
+
+    def slice_copy():
+        return pltpu.make_async_remote_copy(
+            src_ref=outer.at[odd], dst_ref=outer.at[0],
+            send_sem=slice_send_sem, recv_sem=slice_recv_sem,
+            device_id=(section + 1, me), device_id_type=MESH,
+        )
+
+    def slice_arrival():
+        return pltpu.make_async_remote_copy(
+            src_ref=outer.at[0], dst_ref=outer.at[0],
+            send_sem=slice_send_sem, recv_sem=slice_recv_sem,
+            device_id=(section - 1, me), device_id_type=MESH,
+        )
+
+    def stream_rows(q):
+        return pl.ds(pl.multiple_of(q * win, MAIN), win)
+
+    def stream_copy(q):
+        return pltpu.make_async_remote_copy(
+            src_ref=vecs_t.at[stream_rows(q)], dst_ref=vecs.at[stream_rows(q)],
+            send_sem=stream_send_sem.at[q], recv_sem=stream_recv_sem.at[q],
+            device_id=(section + 1, me), device_id_type=MESH,
+        )
+
+    def stream_arrival(q):
+        return pltpu.make_async_remote_copy(
+            src_ref=vecs.at[stream_rows(q)], dst_ref=vecs.at[stream_rows(q)],
+            send_sem=stream_send_sem.at[q], recv_sem=stream_recv_sem.at[q],
+            device_id=(section - 1, me), device_id_type=MESH,
+        )
+
+    chunks = nch // win
+
+    def prepare_odd():
+        for h in range(2):
+            load(h, vecs_t).wait()
+
+        @pl.when(section < last)
+        def _():
+            @pl.loop(0, nch // MAIN)
+            def _(r):
+                part = pl.ds(pl.multiple_of(r * MAIN, MAIN), MAIN)
+                turned = vecs_t[part, win_cols].T
+                outer[0, :, part] = turned[:rows]
+                outer[1, :, part] = turned[rows:]
+            slice_copy().start()
+            slice_copy().wait_send()
+
+        @pl.when(section == 1)
+        def _():
+            for h in range(2):
+                load_too(h).wait()
+
+        @pl.when(section > 1)
+        def _():
+            @pl.loop(0, chunks)
+            def _(q):
+                stream_arrival(q).wait_recv()
+                outer[0] = vecs[pl.ds(pl.multiple_of(q * win, MAIN), rows), :]
+                outer[1] = vecs[pl.ds(pl.multiple_of(q * win + rows, rest), rows), :]
+                for n in range(SIDE):
+                    cols = slice(n * tile, (n + 1) * tile)
+                    block = f_dot(outer[...].reshape(win, nch), vecs_t[:, cols])
+                    vecs[stream_rows(q), cols] = block.astype(bf16)
+        transpose_in_place()
+
+    def near(axis, step):
+        if axis == 0:
+            return ((y + step + SIDE) % SIDE) * SIDE + z
+        return y * SIDE + (z + step + SIDE) % SIDE
+
+    def ring_block(part, group, step):
+        first, second = 1 - part, part
+        shift = {first: 0, second: 0}
+        if group == 0:
+            shift[first] = step
+        else:
+            shift[first] = group - 1
+            shift[second] = step
+        return ((y + shift[0] + SIDE) % SIDE) * SIDE + (z + shift[1] + SIDE) % SIDE
+
+    def ring_copy(part, group, kind, arriving=False):
+        axis = (1 - part) if group == 0 else part
+        origin = (0, 0, -1, 1)[kind]
+        if arriving:
+            origin = (-1, 1, -2, 2)[kind]
+        direction = (1, -1, 1, -1)[kind]
+        start = ring_block(part, group, origin) * rows + (tall if kind == 3 else 0)
+        size = rows if kind < 2 else tall
+        region = vecs.at[pl.ds(pl.multiple_of(start, 32), size), pl.ds(part * half, half)]
+        return pltpu.make_async_remote_copy(
+            src_ref=region, dst_ref=region,
+            send_sem=ring_send_sem.at[part, group, kind],
+            recv_sem=ring_recv_sem.at[part, group, kind],
+            device_id=(section, near(axis, -direction if arriving else direction)),
+            device_id_type=MESH,
+        )
+
+    def ring_pass(part, group):
+        ring_copy(part, group, 0, True).wait_recv()
+        ring_copy(part, group, 2).start()
+        ring_copy(part, group, 1, True).wait_recv()
+        ring_copy(part, group, 3).start()
+
+    def prepare_even():
+        for h in range(2):
+            load(h, vecs).wait()
+
+        @pl.when(section > 0)
+        def _():
+            @pl.loop(0, chunks)
+            def _(q):
+                transpose_chunk(q)
+                stream_copy(q).start()
+
+            slice_arrival().wait_recv()
+            for n in range(SIDE):
+                cols = slice(n * tile, (n + 1) * tile)
+                outer[1, :, cols] = f_dot(outer[0], vecs[:, cols]).astype(bf16)
+            for axis in range(2):
+                for step in (1, -1):
+                    pl.semaphore_signal(
+                        ready_sem, inc=1, device_id=(section, near(axis, step)), device_id_type=MESH
+                    )
+            vecs[pl.ds(pl.multiple_of(me * rows, rest), rows), :] = outer[1]
+            pl.semaphore_wait(ready_sem, 4)
+            for part in range(2):
+                for group in range(2):
+                    for kind in range(2):
+                        ring_copy(part, group, kind).start()
+            for part in range(2):
+                ring_pass(part, 0)
+            for part in range(2):
+                for group in (2, 4):
+                    for kind in range(2):
+                        ring_copy(part, group, kind).start()
+            for part in range(2):
+                ring_pass(part, 1)
+            for part in range(2):
+                for kind in (2, 3):
+                    ring_copy(part, 0, kind, True).wait_recv()
+                for kind in range(2):
+                    ring_copy(part, 3, kind).start()
+            for group in (2, 4, 3):
+                for part in range(2):
+                    ring_pass(part, group)
+            for group in range(1, 5):
+                for part in range(2):
+                    for kind in (2, 3):
+                        ring_copy(part, group, kind, True).wait_recv()
+            for part in range(2):
+                for group in range(5):
+                    for kind in range(4):
+                        ring_copy(part, group, kind).wait_send()
+
+            @pl.loop(0, chunks)
+            def _(q):
+                stream_copy(q).wait_send()
 
     def block_copy(trip, slot, place, dest):
         return pltpu.make_async_remote_copy(
@@ -132,7 +356,7 @@
         )
 
     def ship(trip, slot, step, value):
-        main_t = value[:MAIN].T
+        main_t = value[:MAIN].astype(bf16).T
         rest_t = value[rest:].T
         for j in range(SIDE):
             base = rows * j
@@ -146,7 +370,7 @@
                 bottom = jnp.concatenate([rest_t[base + rest + tall:base + rows], rest_t[base:base + rest]], 0)
             packed = jnp.where(low, pltpu.roll(top, rest, 1), bottom)
             place = SIDE * step + j
-            send[slot, place, :rows] = main.astype(bf16)
+            send[slot, place, :rows] = main
             send[slot, place, rows:] = packed.astype(bf16)
         for j in range(SIDE):
             place = SIDE * step + j
@@ -159,6 +383,16 @@
                     block_copy(trip, slot, place, dest).start()
         if step == SIDE - 1:
             recv[trip, slot, me] = send[slot, SIDE * step + z]
+
+    def tile_cols(step):
+        return pl.ds(pl.multiple_of(y_order[step] * tile, MAIN), tile)
+
+    def ship_all(trip, slot, product):
+        value = product(0)
+        for step in range(SIDE):
+            after = product(step + 1) if step < SIDE - 1 else None
+            ship(trip, slot, step, value)
+            value = after
 
     def wait_sent(trip, slot):
         for place in range(MATS):
@@ -197,10 +431,10 @@
     def half_rows(which):
         return pl.ds(pl.multiple_of(which * half, MAIN), half)
 
-    def pass_copy(slot, n):
+    def pass_copy(slot, n, source):
         part = pl.ds(n * tile, tile)
         return pltpu.make_async_remote_copy(
-            src_ref=rmat.at[slot, :, part],
+            src_ref=source.at[slot, :, part],
             dst_ref=rmat.at[slot, :, part],
             send_sem=pass_send_sem.at[slot, n],
             recv_sem=pass_recv_sem.at[slot, n],
@@ -235,10 +469,12 @@
                 for n in range(2):
                     cols = slice(n * half, (n + 1) * half)
                     inner[slot, :, cols] = dot(rmat[slot, :, :half], vecs[:half, cols])
-        for step in range(SIDE):
-            cols = pl.ds(pl.multiple_of(y_order[step] * tile, MAIN), tile)
-            value = inner[slot, :, cols] + dot(rmat[slot, :, half:], vecs[half:, cols])
-            ship(0, slot, step, value)
+
+        def product(step):
+            cols = tile_cols(step)
+            return inner[slot, :, cols] + dot(rmat[slot, :, half:], vecs[half:, cols])
+
+        ship_all(0, slot, product)
 
     def diag_copy(slot, dest):
         return pltpu.make_async_remote_copy(
@@ -266,9 +502,12 @@
             cols = slice(n * half, (n + 1) * half)
             inner[slot, :, cols] = dot(half_lhs[...], vecs[half_rows(far_half), cols])
         gather_half(0, slot, own_half, True)
-        for n in range(2):
-            cols = slice(n * half, (n + 1) * half)
+
+        def finish(step):
+            cols = tile_cols(step)
             inner[slot, :, cols] += dot(half_lhs[...], vecs[half_rows(own_half), cols])
+
+        finish(SIDE - 1)
         mine = jnp.sum(jnp.where(on_diag, inner[slot, :, win_cols], 0.0), axis=0, keepdims=True)
         diag_send[slot] = jnp.zeros(diag_send.shape[1:], f32)
         for n in range(win // MAIN):
@@ -281,7 +520,10 @@
             def _():
                 diag_copy(slot, dest).start()
 
-    def right_half(slot):
+        for step in range(SIDE - 1):
+            finish(step)
+
+    def propagate(slot):
         @pl.loop(0, MATS)
         def _(source):
             @pl.when(source != me)
@@ -293,8 +535,8 @@
             pair = diag_recv[slot, 2 * p] + diag_recv[slot, 2 * p + 1]
             pieces += [pair[n:n + 1, :] for n in range(win // MAIN)]
         full_diag = jnp.concatenate(pieces, axis=1)
-        g_one = g_one_ref[slot:slot + 1, :]
-        g_two = g_two_ref[slot:slot + 1, :]
+        g_one = g_one_ref[pl.ds(slot, 1), :]
+        g_two = g_two_ref[pl.ds(slot, 1), :]
         precond = 1.0 / (g_one + jnp.abs(full_diag))
         side = g_two * precond
         term = g_one - 2.0 * g_two * g_two * precond + g_one * side * side
@@ -303,15 +545,42 @@
         side_win = side_ref[0:1, win_cols]
         term_win = side_ref[1:2, win_cols]
         side_rows = jnp.sum(jnp.where(on_diag, side_win, 0.0), axis=1, keepdims=True)
+        scaled = side_rows * inner[slot, :, win_cols] * side_win
+        outer[slot, :, win_cols] = (scaled + jnp.where(on_diag, term_win, 0.0)).astype(bf16)
         for q in range(nch // win):
             cols = slice(q * win, (q + 1) * win)
-            outer[:, cols] = (side_rows * inner[slot, :, cols] * side[:, cols]).astype(bf16)
-        scaled = side_rows * inner[slot, :, win_cols] * side_win
-        outer[:, win_cols] = (scaled + jnp.where(on_diag, term_win, 0.0)).astype(bf16)
+
+            @pl.when(q != me // 2)
+            def _():
+                outer[slot, :, cols] = (side_rows * inner[slot, :, cols] * side[:, cols]).astype(bf16)
+
+            if q % 2 == 1:
+                @pl.when((section > 0) & (section < last))
+                def _():
+                    pass_copy(slot, q // 2, outer).start()
+
+        @pl.when((section % 2 == 1) & (section > 1) & (section < last) & (slot == 1))
+        def _():
+            pl.semaphore_signal(go_sem, inc=1, device_id=(section - 1, me), device_id_type=MESH)
+
+    def flip_out(slot):
+        @pl.when((slot == 0) & (section < last - 1))
+        def _():
+            pl.semaphore_wait(go_sem, 1)
+
+        for n in range(SIDE):
+            pass_copy(slot, n, outer).wait_send()
         wait_sent(0, slot)
-        for step in range(SIDE):
-            cols = pl.ds(pl.multiple_of(y_order[step] * tile, MAIN), tile)
-            ship(1, slot, step, dot(outer[...], vecs_t[:, cols]))
+        ship_all(2, slot, lambda step: outer[slot, :, tile_cols(step)].astype(f32))
+
+    def flip_in(slot):
+        for which, own in ((far_half, False), (own_half, True)):
+            gather_half(2, slot, which, own)
+            outer[slot, :, half_rows(which)] = half_lhs[...]
+
+    def right_half(slot):
+        wait_sent(1, slot)
+        ship_all(1, slot, lambda step: dot(outer[slot], vecs_t[:, tile_cols(step)]))
 
     def next_rows(slot):
         gather_half(1, slot, far_half, False)
@@ -324,34 +593,49 @@
             value = inner[slot, :, cols] + dot(half_lhs[...], vecs_t[half_rows(own_half), cols])
             rmat[slot, :, cols] = value.astype(bf16)
 
-            @pl.when(section < sections - 1)
+            @pl.when(section == 0)
             def _():
-                pass_copy(slot, n).start()
+                pass_copy(slot, n, rmat).start()
         for copy in out_copies(slot):
             copy.start()
 
-    for h in range(2):
-        load(h).wait()
-
-    @pl.when(section > 0)
+    @pl.when(even_section)
     def _():
-        transpose_vecs()
-
-    left_half(0)
-
-    @pl.when(section == 0)
+        prepare_even()
+
+    @pl.when(section % 2 == 1)
     def _():
-        transpose_vecs()
-
-    inner_product(0)
-    left_half(1)
-    right_half(0)
-    inner_product(1)
-    next_rows(0)
-    right_half(1)
-    next_rows(1)
-
-    for slot in range(2):
+        prepare_odd()
+
+    def turn(part):
+        @pl.loop(part * (chunks // 2), (part + 1) * (chunks // 2))
+        def _(q):
+            transpose_chunk(q)
+
+    stages = [left_half, inner_product, propagate, right_half, next_rows, flip_out, flip_in, turn]
+    is_first = 1 - (section + last) // sections
+    is_last = section // last
+    is_flipped = (1 - section % 2) * (1 - is_first)
+    is_plain = 1 - is_first - is_last - is_flipped
+    now, later = (
+        is_first * a + is_last * b + is_flipped * c + is_plain * d
+        for a, b, c, d in zip(*(digits(order) for order in (FIRST, LAST, FLIPPED, PLAIN)))
+    )
+
+    def step(_, queue):
+        now, later = queue
+        code = now % BASE
+        stage, slot = code // 2, code % 2
+        for n, run in enumerate(stages):
+            @pl.when(stage == n)
+            def _():
+                run(slot)
+        return now // BASE + (later % BASE) * BASE ** (DIGITS - 1), later // BASE
+
+    lax.fori_loop(0, STEPS, step, (now, later))
+
+    @pl.loop(0, 2)
+    def _(slot):
         wait_sent(1, slot)
         for copy in out_copies(slot):
             copy.wait()
@@ -362,10 +646,10 @@
             def _():
                 diag_copy(slot, dest).wait_send()
 
-        @pl.when(section < sections - 1)
+        @pl.when((section < last) & jnp.logical_not(flipped))
         def _():
             for n in range(SIDE):
-                pass_copy(slot, n).wait_send()
+                pass_copy(slot, n, rmat).wait_send()
 
 
 def on_device(sections, eigvec, eig_level, energies, order, init_r):
@@ -388,22 +672,30 @@
             pltpu.VMEM((nch, nch), bf16),
             pltpu.VMEM((2, rows, nch), bf16),
             pltpu.VMEM((2, rows, nch), f32),
-            pltpu.VMEM((rows, nch), bf16),
+            pltpu.VMEM((2, rows, nch), bf16),
             pltpu.VMEM((rows, nch // 2), bf16),
             pltpu.VMEM((2, MATS, block, MAIN), bf16),
-            pltpu.VMEM((2, 2, MATS, block, MAIN), bf16),
+            pltpu.VMEM((3, 2, MATS, block, MAIN), bf16),
             pltpu.VMEM((2, 8, MAIN), f32),
             pltpu.VMEM((2, MATS, 8, MAIN), f32),
             pltpu.VMEM((2, nch), f32),
-            dma((2,)),
+            dma((4,)),
             dma((2, 2)),
             dma((2, 2)),
             dma((2, MATS)),
-            dma((2, 2, MATS)),
+            dma((3, 2, MATS)),
             dma((2, MATS)),
             dma((2, MATS)),
             dma((2, SIDE)),
             dma((2, SIDE)),
+            dma(()),
+            dma(()),
+            dma((nch // (2 * rows),)),
+            dma((nch // (2 * rows),)),
+            dma((2, 5, SIDE)),
+            dma((2, 5, SIDE)),
+            pltpu.SemaphoreType.REGULAR,
+            pltpu.SemaphoreType.REGULAR,
         ],
         compiler_params=pltpu.CompilerParams(
             collective_id=0, has_side_effects=True, vmem_limit_bytes=67043328

time: 457 us -> 358 us (0.78)
  Pallas kernels: 445 us -> 347 us
    pallas_call x1, Pallas kernels: 445 us -> 347 us  [on_device(): pl.pallas_call(functools.partial(kernel, sections), out_shape=jax.ShapeDt...]
where the time goes in v2:
time: 358 us
  Pallas kernels  347 us (97%)
  local copies, waits for them, and re-layouts  6.88 us (2%)
  other arithmetic  4.54 us (1%)
    pallas_call x1, Pallas kernels, on_device(): pl.pallas_call(functools.partial(kernel, sections), out_shape=jax.ShapeDt...  347 us

profile of v2, /device:TPU:7, one launch (start us, length us, event | category | flops | bytes accessed | tf_op | source)
XLA Modules:
  0.0 358.1 jit_solution(3430430670234711664)
XLA Ops:
  0.0 0.7 compare_select_fusion.1
  0.7 1.3 gather_fusion
  2.0 0.7 broadcast_select_fusion.1
  2.6 1.5 broadcast_divide_fusion
  4.1 2.4 gather_fusion.1
  6.5 1.7 broadcast_select_fusion.init_ref
  8.2 346.6 %sectors.1 = bf16[1,2,192,3072]{3,2,1,0:T(8,128)(2,1)} custom-call(bf16[1,3072,3072]{2,1,0:T(8,128)(2,1)} %eig_ref.1, f32[2,3072]{1,0:T(2,128)} %get-tuple-element.8.g_one_ref, f32[2,3072]{1,0:T(2,128)} %get-tuple-element.7.g_two_ref, bf16[2,192,3072]{2,1,0:T(8,128)(2,1)} %broadcast_select_fusion.init_ref), custom_call_target="tpu_custom_call" | custom-call | tf_op jit(solution)/shard_map/sectors/pallas_call | solution.py:665
  354.9 3.2 copy.7
  (1 shorter events, 0.0 us)

commit v3 on v2

--- a/solution.py
+++ b/solution.py
@@ -22,7 +22,7 @@
 CHAIN = [
     (LEFT, 0), (INNER, 0), (PROPAGATE, 0), (LEFT, 1), (INNER, 1), (PROPAGATE, 1),
 ]
-PLAIN = CHAIN + [(RIGHT, 0), (RIGHT, 1), (NEXT, 0), (NEXT, 1)]
+PLAIN = CHAIN + [(TURN, 0), (RIGHT, 0), (RIGHT, 1), (NEXT, 0), (NEXT, 1)]
 FLIPPED = CHAIN + [
     (FLIP_OUT, 0), (FLIP_OUT, 1), (FLIP_IN, 0), (RIGHT, 0), (FLIP_IN, 1), (RIGHT, 1),
     (NEXT, 0), (NEXT, 1),
@@ -54,11 +54,11 @@
 
 def kernel(
     sections,
-    eig_ref, g_one_ref, g_two_ref, init_ref, out_ref,
+    eig_ref, g_one_ref, g_two_ref, init_ref, order_ref, out_ref,
     vecs, vecs_t, rmat, inner, outer, half_lhs, send, recv, diag_send, diag_recv, side_ref,
     load_sem, init_sem, out_sem, send_sem, recv_sem, diag_send_sem, diag_recv_sem,
     pass_send_sem, pass_recv_sem, slice_send_sem, slice_recv_sem, stream_send_sem, stream_recv_sem,
-    ring_send_sem, ring_recv_sem, ready_sem, go_sem,
+    ring_send_sem, ring_recv_sem, ready_sem, go_sem, clear_sem,
 ):
     nch = vecs.shape[0]
     rows = rmat.shape[1]
@@ -74,12 +74,10 @@
     y, z = me // SIDE, me % SIDE
     odd = me % 2
     y_order = [(y + 2) % SIDE, SIDE - 1 - y, y + 1 - 2 * (y % 2), y]
-    own_half = y // 2
-    far_half = 1 - own_half
-
     even_section = section % 2 == 0
     flipped = even_section & (section >= 2)
     last = sections - 1
+    late_turn = 3
     f_dot = functools.partial(jnp.dot, preferred_element_type=f32)
 
     def load(h, space):
@@ -112,7 +110,7 @@
 
     def init_copies(slot):
         return [
-            pltpu.make_async_copy(init_ref.at[slot, a], rmat.at[slot, b], init_sem.at[slot, n])
+            pltpu.make_async_copy(init_ref.at[slot, a], outer.at[slot, b], init_sem.at[slot, n])
             for n, (a, b) in enumerate(row_copies(slot))
         ]
 
@@ -156,13 +154,11 @@
     on_diag = col_id == target
     win_cols = pl.ds(pl.multiple_of((me // 2) * win, MAIN), win)
 
-    def transpose_chunk(q):
-        cols = pl.ds(pl.multiple_of(q * win, MAIN), win)
-
-        @pl.loop(0, nch // MAIN)
+    def transpose_rows(first, count):
+        @pl.loop(first, first + count)
         def _(r):
             part = pl.ds(pl.multiple_of(r * MAIN, MAIN), MAIN)
-            vecs_t[cols, part] = vecs[part, cols].T
+            vecs_t[:, part] = vecs[part, :].T
 
     def transpose_in_place(block=256):
         @pl.loop(0, nch // block)
@@ -240,7 +236,10 @@
                     cols = slice(n * tile, (n + 1) * tile)
                     block = f_dot(outer[...].reshape(win, nch), vecs_t[:, cols])
                     vecs[stream_rows(q), cols] = block.astype(bf16)
-        transpose_in_place()
+
+        @pl.when(section != late_turn)
+        def _():
+            transpose_in_place()
 
     def near(axis, step):
         if axis == 0:
@@ -281,14 +280,23 @@
         ring_copy(part, group, 3).start()
 
     def prepare_even():
+        @pl.when(section == 0)
+        def _():
+            for slot in range(2):
+                for copy in init_copies(slot):
+                    copy.wait()
+            for slot in range(2):
+                rmat[slot] = jnp.where(order_ref[slot] == 0, outer[0], outer[1])
+
         for h in range(2):
             load(h, vecs).wait()
 
         @pl.when(section > 0)
         def _():
+            transpose_rows(0, nch // MAIN)
+
             @pl.loop(0, chunks)
             def _(q):
-                transpose_chunk(q)
                 stream_copy(q).start()
 
             slice_arrival().wait_recv()
@@ -404,32 +412,33 @@
                 def _():
                     block_copy(trip, slot, place, dest).wait_send()
 
-    def gather_half(trip, slot, which, own):
-        for n in range(MATS // 2):
-            source = which * (MATS // 2) + n
+    def gather_group(trip, slot, group, own):
+        for n in range(SIDE):
+            source = group * SIDE + n
             if own:
                 @pl.when(source != me)
                 def _():
                     block_arrival(trip, slot, source).wait_recv()
             else:
                 block_arrival(trip, slot, source).wait_recv()
-        for q in range(MATS // 4):
-            even = which * (MATS // 2) + 2 * q
-            base = win * q
-            half_lhs[:, base:base + MAIN] = recv[trip, slot, even, :rows]
-            half_lhs[:, base + 2 * MAIN:base + 3 * MAIN] = recv[trip, slot, even + 1, :rows]
+        for q in range(SIDE // 2):
+            even = group * SIDE + 2 * q
+            at = pl.multiple_of(group * tile + win * q, MAIN)
+            half_lhs[:, pl.ds(at, MAIN)] = recv[trip, slot, even, :rows]
+            half_lhs[:, pl.ds(at + 2 * MAIN, MAIN)] = recv[trip, slot, even + 1, :rows]
             left = recv[trip, slot, even, rows:].astype(f32)
             right = recv[trip, slot, even + 1, rows:].astype(f32)
             top = jnp.where(low, left, pltpu.roll(right, rest, 1))
             bottom = jnp.where(low, pltpu.roll(left, rest, 1), right)
-            half_lhs[:tall, base + MAIN:base + 2 * MAIN] = top.astype(bf16)
-            half_lhs[tall:, base + MAIN:base + 2 * MAIN] = bottom.astype(bf16)
+            half_lhs[:tall, pl.ds(at + MAIN, MAIN)] = top.astype(bf16)
+            half_lhs[tall:, pl.ds(at + MAIN, MAIN)] = bottom.astype(bf16)
+
+    def gather(trip, slot):
+        for step in range(SIDE):
+            gather_group(trip, slot, y_order[step], step == SIDE - 1)
 
     def dot(a, b):
         return jnp.dot(a, b, preferred_element_type=f32)
-
-    def half_rows(which):
-        return pl.ds(pl.multiple_of(which * half, MAIN), half)
 
     def pass_copy(slot, n, source):
         part = pl.ds(n * tile, tile)
@@ -454,25 +463,17 @@
         )
 
     def left_half(slot):
-        @pl.when(section == 0)
-        def _():
-            for copy in init_copies(slot):
-                copy.wait()
-
-        for h in range(2):
-            @pl.when(section > 0)
-            def _():
-                for n in range(2 * h, 2 * h + 2):
-                    pass_arrival(slot, n).wait_recv()
-
-            if h == 0:
-                for n in range(2):
-                    cols = slice(n * half, (n + 1) * half)
-                    inner[slot, :, cols] = dot(rmat[slot, :, :half], vecs[:half, cols])
+        @pl.when(flipped & (slot == 1))
+        def _():
+            pl.semaphore_wait(clear_sem, 1)
+
+        @pl.when(section > 0)
+        def _():
+            for n in range(SIDE):
+                pass_arrival(slot, n).wait_recv()
 
         def product(step):
-            cols = tile_cols(step)
-            return inner[slot, :, cols] + dot(rmat[slot, :, half:], vecs[half:, cols])
+            return dot(rmat[slot], vecs[:, tile_cols(step)])
 
         ship_all(0, slot, product)
 
@@ -497,15 +498,15 @@
         )
 
     def inner_product(slot):
-        gather_half(0, slot, far_half, False)
-        for n in range(2):
-            cols = slice(n * half, (n + 1) * half)
-            inner[slot, :, cols] = dot(half_lhs[...], vecs[half_rows(far_half), cols])
-        gather_half(0, slot, own_half, True)
+        gather(0, slot)
+
+        @pl.when((section % 2 == 1) & (section > 1) & (slot == 0))
+        def _():
+            pl.semaphore_signal(clear_sem, inc=1, device_id=(section - 1, me), device_id_type=MESH)
 
         def finish(step):
             cols = tile_cols(step)
-            inner[slot, :, cols] += dot(half_lhs[...], vecs[half_rows(own_half), cols])
+            inner[slot, :, cols] = dot(half_lhs[...], vecs[:, cols])
 
         finish(SIDE - 1)
         mine = jnp.sum(jnp.where(on_diag, inner[slot, :, win_cols], 0.0), axis=0, keepdims=True)
@@ -574,23 +575,18 @@
         ship_all(2, slot, lambda step: outer[slot, :, tile_cols(step)].astype(f32))
 
     def flip_in(slot):
-        for which, own in ((far_half, False), (own_half, True)):
-            gather_half(2, slot, which, own)
-            outer[slot, :, half_rows(which)] = half_lhs[...]
+        gather(2, slot)
+        outer[slot] = half_lhs[...]
 
     def right_half(slot):
         wait_sent(1, slot)
         ship_all(1, slot, lambda step: dot(outer[slot], vecs_t[:, tile_cols(step)]))
 
     def next_rows(slot):
-        gather_half(1, slot, far_half, False)
-        for n in range(2):
-            cols = slice(n * half, (n + 1) * half)
-            inner[slot, :, cols] = dot(half_lhs[...], vecs_t[half_rows(far_half), cols])
-        gather_half(1, slot, own_half, True)
+        gather(1, slot)
         for n in range(SIDE):
             cols = slice(n * tile, (n + 1) * tile)
-            value = inner[slot, :, cols] + dot(half_lhs[...], vecs_t[half_rows(own_half), cols])
+            value = dot(half_lhs[...], vecs_t[:, cols])
             rmat[slot, :, cols] = value.astype(bf16)
 
             @pl.when(section == 0)
@@ -608,9 +604,13 @@
         prepare_odd()
 
     def turn(part):
-        @pl.loop(part * (chunks // 2), (part + 1) * (chunks // 2))
-        def _(q):
-            transpose_chunk(q)
+        @pl.when(section == 0)
+        def _():
+            transpose_rows(part * (nch // MAIN // 2), nch // MAIN // 2)
+
+        @pl.when(section == late_turn)
+        def _():
+            transpose_in_place()
 
     stages = [left_half, inner_product, propagate, right_half, next_rows, flip_out, flip_in, turn]
     is_first = 1 - (section + last) // sections
@@ -655,8 +655,8 @@
 def on_device(sections, eigvec, eig_level, energies, order, init_r):
     nch = eigvec.shape[1]
     rows = init_r.shape[1]
-    g_one, g_two = greens(eig_level[0][None, :], jnp.take(energies, order)[:, None])
-    initial = jnp.take(init_r, order, axis=0)
+    taken = jnp.where(order == 0, energies[0], energies[1])
+    g_one, g_two = greens(eig_level[0][None, :], taken[:, None])
     any_spec = pl.BlockSpec(memory_space=pl.ANY)
     vmem_spec = pl.BlockSpec(memory_space=pltpu.VMEM)
     dma = pltpu.SemaphoreType.DMA
@@ -665,7 +665,7 @@
     return pl.pallas_call(
         functools.partial(kernel, sections),
         out_shape=jax.ShapeDtypeStruct((1, 2, rows, nch), bf16),
-        in_specs=[any_spec, vmem_spec, vmem_spec, any_spec],
+        in_specs=[any_spec, vmem_spec, vmem_spec, any_spec, pl.BlockSpec(memory_space=pltpu.SMEM)],
         out_specs=any_spec,
         scratch_shapes=[
             pltpu.VMEM((nch, nch), bf16),
@@ -673,7 +673,7 @@
             pltpu.VMEM((2, rows, nch), bf16),
             pltpu.VMEM((2, rows, nch), f32),
             pltpu.VMEM((2, rows, nch), bf16),
-            pltpu.VMEM((rows, nch // 2), bf16),
+            pltpu.VMEM((rows, nch), bf16),
             pltpu.VMEM((2, MATS, block, MAIN), bf16),
             pltpu.VMEM((3, 2, MATS, block, MAIN), bf16),
             pltpu.VMEM((2, 8, MAIN), f32),
@@ -696,12 +696,13 @@
             dma((2, 5, SIDE)),
             pltpu.SemaphoreType.REGULAR,
             pltpu.SemaphoreType.REGULAR,
+            pltpu.SemaphoreType.REGULAR,
         ],
         compiler_params=pltpu.CompilerParams(
             collective_id=0, has_side_effects=True, vmem_limit_bytes=67043328
         ),
         name="sectors",
-    )(eigvec, g_one, g_two, initial)
+    )(eigvec, g_one, g_two, init_r, order)
 
 
 def solution(mesh):

time: 358 us -> 345 us (0.964)
  Pallas kernels: 347 us -> 336 us
    pallas_call x1, Pallas kernels: 347 us -> 336 us  [on_device(): pl.pallas_call(functools.partial(kernel, sections), out_shape=jax.ShapeDt...]
    gather x2 -> x0, local copies, waits for them, and re-layouts: 3.65 us -> none  [the longest x1 2.36 us: on_device(): initial = jnp.take(init_r, order, axis=0)]
where the time goes in v3:
time: 345 us; the launch traced here: 344 us
  Pallas kernels  336 us (97%)
  local copies, waits for them, and re-layouts  4.56 us (1%)
  other arithmetic  3.45 us (1%)
    pallas_call x1, Pallas kernels, on_device(): pl.pallas_call(functools.partial(kernel, sections), out_shape=jax.ShapeDt...  336 us

profile of v3, /device:TPU:7, one launch (start us, length us, event | category | flops | bytes accessed | tf_op | source)
XLA Modules:
  0.0 344.0 jit_solution(6874616624471341020)
XLA Ops:
  0.0 1.3 fusion.2
  1.3 1.9 compare_select_fusion.1
  3.3 1.5 broadcast_divide_fusion
  4.8 336.0 %sectors.1 = bf16[1,2,192,3072]{3,2,1,0:T(8,128)(2,1)} custom-call(bf16[1,3072,3072]{2,1,0:T(8,128)(2,1)} %eig_ref.1, f32[2,3072]{1,0:T(2,128)} %get-tuple-element.6.g_one_ref, f32[2,3072]{1,0:T(2,128)} %get-tuple-element.5.g_two_ref, bf16[2,192,3072]{2,1,0:T(8,128)(2,1)} %init_ref.1, s32[2]{0:T(128)} %order_ref.1), custom_call_target="tpu_custom_call" | custom-call | tf_op jit(solution)/shard_map/sectors/pallas_call | solution.py:665
  340.8 3.2 copy.7

commit v4 on v3

--- a/solution.py
+++ b/solution.py
@@ -22,14 +22,14 @@
 CHAIN = [
     (LEFT, 0), (INNER, 0), (PROPAGATE, 0), (LEFT, 1), (INNER, 1), (PROPAGATE, 1),
 ]
-PLAIN = CHAIN + [(TURN, 0), (RIGHT, 0), (RIGHT, 1), (NEXT, 0), (NEXT, 1)]
+PLAIN = CHAIN + [(RIGHT, 0), (RIGHT, 1), (NEXT, 0), (NEXT, 1)]
 FLIPPED = CHAIN + [
     (FLIP_OUT, 0), (FLIP_OUT, 1), (FLIP_IN, 0), (RIGHT, 0), (FLIP_IN, 1), (RIGHT, 1),
     (NEXT, 0), (NEXT, 1),
 ]
 LAST = [
-    (LEFT, 0), (INNER, 0), (PROPAGATE, 0), (LEFT, 1), (RIGHT, 0), (INNER, 1), (NEXT, 0),
-    (PROPAGATE, 1), (RIGHT, 1), (NEXT, 1),
+    (LEFT, 0), (INNER, 0), (PROPAGATE, 0), (LEFT, 1), (RIGHT, 0), (INNER, 1), (PROPAGATE, 1),
+    (RIGHT, 1), (NEXT, 0), (NEXT, 1),
 ]
 STEPS, BASE, DIGITS = 14, 17, 7
 
@@ -77,7 +77,6 @@
     even_section = section % 2 == 0
     flipped = even_section & (section >= 2)
     last = sections - 1
-    late_turn = 3
     f_dot = functools.partial(jnp.dot, preferred_element_type=f32)
 
     def load(h, space):
@@ -236,10 +235,7 @@
                     cols = slice(n * tile, (n + 1) * tile)
                     block = f_dot(outer[...].reshape(win, nch), vecs_t[:, cols])
                     vecs[stream_rows(q), cols] = block.astype(bf16)
-
-        @pl.when(section != late_turn)
-        def _():
-            transpose_in_place()
+        transpose_in_place()
 
     def near(axis, step):
         if axis == 0:
@@ -604,13 +600,7 @@
         prepare_odd()
 
     def turn(part):
-        @pl.when(section == 0)
-        def _():
-            transpose_rows(part * (nch // MAIN // 2), nch // MAIN // 2)
-
-        @pl.when(section == late_turn)
-        def _():
-            transpose_in_place()
+        transpose_rows(part * (nch // MAIN // 2), nch // MAIN // 2)
 
     stages = [left_half, inner_product, propagate, right_half, next_rows, flip_out, flip_in, turn]
     is_first = 1 - (section + last) // sections

time: 345 us -> 338 us (0.980)
  Pallas kernels: 336 us -> 328 us
    pallas_call x1, Pallas kernels: 336 us -> 328 us  [on_device(): pl.pallas_call(functools.partial(kernel, sections), out_shape=jax.ShapeDt...]
where the time goes in v4:
time: 338 us; the launch traced here: 336 us
  Pallas kernels  328 us (97%)
  local copies, waits for them, and re-layouts  4.56 us (1%)
  other arithmetic  3.45 us (1%)
    pallas_call x1, Pallas kernels, on_device(): pl.pallas_call(functools.partial(kernel, sections), out_shape=jax.ShapeDt...  328 us

profile of v4, /device:TPU:7, one launch (start us, length us, event | category | flops | bytes accessed | tf_op | source)
XLA Modules:
  0.0 336.0 jit_solution(5847822931462925865)
XLA Ops:
  0.0 1.3 fusion.2
  1.3 1.9 compare_select_fusion.1
  3.3 1.5 broadcast_divide_fusion
  4.8 328.0 %sectors.1 = bf16[1,2,192,3072]{3,2,1,0:T(8,128)(2,1)} custom-call(bf16[1,3072,3072]{2,1,0:T(8,128)(2,1)} %eig_ref.1, f32[2,3072]{1,0:T(2,128)} %get-tuple-element.6.g_one_ref, f32[2,3072]{1,0:T(2,128)} %get-tuple-element.5.g_two_ref, bf16[2,192,3072]{2,1,0:T(8,128)(2,1)} %init_ref.1, s32[2]{0:T(128)} %order_ref.1), custom_call_target="tpu_custom_call" | custom-call | tf_op jit(solution)/shard_map/sectors/pallas_call | solution.py:655
  332.8 3.2 copy.7
